TPU v7x, 512 devices: a whole 4x4x16 slice. The times are simulated.
512 devices in a mesh: mem: 4 (over x), col: 128 (over z, y, core).
Axes of the slice: x: 4, y: 4, z: 16, core: 2. Of those that a mesh axis runs over, the one named last changes fastest.
Arguments:
- adj_final: float32 [16, 137, 65536], P('mem', None, 'col'), parts along dimension 0, may hold values from -60 to 60
- inverses: float32 [8, 512, 137, 137], P('mem', 'col'), parts along dimension 0, may hold values from 0 to 1
- dep_lists: int32 [8, 512, 5], P('mem', 'col'), parts along dimension 0, may hold values from 0 to 511, as said below
- dep_points: int32 [8, 4, 65536], P('mem', None, 'col'), parts along dimension 0, may hold values from 0 to 639, as said below
- weights: float32 [8, 4, 65536], P('mem', None, 'col'), parts along dimension 0, may hold values from 0 to 1, as said below
Outputs:
- adj_mid: float32 [16, 137, 65536], P('mem', None, 'col'), parts along dimension 0
- lanczos: float32 [16, 137, 65536], P('mem', None, 'col'), parts along dimension 0
There are 4 independent parts, one for each index of `mem`. A program takes and returns all parts, laid end to end along the dimension named above; each array names one. Nothing has to cross between parts.
Inputs may be any that keep to these rules, and one draw needn't show every extreme that they name: `dep_lists`: every entry of a block's list is a block within 2 blocks of that block, counting cyclically over all 512 blocks; the list's first entries are distinct and the rest repeat the block itself. `dep_points`: the slot of every point indexes one of the first entries of its arrival block's list. The 4 weights of a column are bilinear weights and sum to one.
All inputs are finite; a program needn't handle non-finite values.
Results may differ from a plain program's by a relative error of at most 0.0003.
Values sent between devices are 32-bit elements; how exact they have to be, the bound alone decides.
A program may use at most 64 MiB of HBM per device.

v0:
```python
import jax
import jax.numpy as jnp
from jax import lax
from jax.sharding import PartitionSpec as P

BCOLS = 128
REACH = 2
SLOTS = 5
POINTS = 4
STEPS = 2


eps_energy = 1e-06


def passed_along(value, axis, steps):
    count = lax.axis_size(axis)
    pairs = [(source, (source + steps) % count) for source in range(count)]
    return lax.ppermute(value, axis, pairs)


def slot_matrix(block_points, block_weights, slot_number):
    slot_ids = block_points // BCOLS
    within = block_points % BCOLS
    chosen = jnp.where(slot_ids == slot_number, block_weights, 0.0)
    columns = lax.broadcasted_iota(jnp.int32, (1, 1, BCOLS), 2)
    one_hot = (within[:, :, None] == columns).astype(jnp.float32)
    return jnp.sum(one_hot * chosen[:, :, None], axis=0)


def add_block(accumulated, block_rows, block_points, block_weights, route_row, locate, slot_limit):

    def one_slot(slot_number, current):
        matrix = slot_matrix(block_points, block_weights, slot_number)
        partial_block = jnp.dot(
            block_rows, matrix, precision=lax.Precision.HIGHEST, preferred_element_type=jnp.float32
        )
        position, inside = locate(route_row[slot_number])
        previous = lax.dynamic_slice_in_dim(current, position, 1, 1)
        return lax.dynamic_update_slice_in_dim(
            current, previous + inside * partial_block[:, None, :], position, 1
        )

    return lax.fori_loop(0, slot_limit, one_slot, accumulated)


def over_blocks(
    accumulated, rows_all, point_blocks, weight_blocks, route_table, block_total, locate
):

    def one_block(block_index, current):
        block_rows = lax.dynamic_index_in_dim(rows_all, block_index, 1, keepdims=False)
        block_points = lax.dynamic_index_in_dim(point_blocks, block_index, 1, keepdims=False)
        block_weights = lax.dynamic_index_in_dim(weight_blocks, block_index, 1, keepdims=False)
        route_row = lax.dynamic_index_in_dim(route_table, block_index, 0, keepdims=False)
        slot_limit = SLOTS
        return add_block(
            current, block_rows, block_points, block_weights, route_row, locate, slot_limit
        )

    return lax.fori_loop(0, block_total, one_block, accumulated)


def spread(adjoint, inverse, routes, points, weights):
    variables, levels, col_count = adjoint.shape
    block_count = col_count // BCOLS
    row_count = variables * levels
    all_blocks = lax.axis_size("col") * block_count
    first_block = lax.axis_index("col") * block_count
    blocked = adjoint.reshape(variables, levels, block_count, BCOLS)
    diffused = jnp.einsum("blk,vlbc->vkbc", inverse, blocked, precision=lax.Precision.HIGHEST)
    diffused = diffused.reshape(row_count, block_count, BCOLS)
    point_blocks = points.reshape(POINTS, block_count, BCOLS)
    weight_blocks = weights.reshape(POINTS, block_count, BCOLS)

    def locate_near(target):
        return ((target - first_block + REACH) % all_blocks, 1.0)

    extended = jnp.zeros((row_count, block_count + 2 * REACH, BCOLS), jnp.float32)
    extended = over_blocks(
        extended, diffused, point_blocks, weight_blocks, routes, block_count, locate_near
    )
    from_below = passed_along(extended[:, block_count + REACH :], "col", 1)
    from_above = passed_along(extended[:, :REACH], "col", -1)
    owned = extended[:, REACH : REACH + block_count]
    owned = owned.at[:, :REACH].add(from_below)
    owned = owned.at[:, block_count - REACH :].add(from_above)
    return owned.reshape(variables, levels, col_count)


def shards(adj_final, inverses, dep_lists, dep_points, weights):
    adjoint = adj_final
    adj_mid = adj_final
    for step_index in range(STEPS - 1, -1, -1):
        adjoint = spread(
            adjoint,
            inverses[step_index],
            dep_lists[step_index],
            dep_points[step_index],
            weights[step_index],
        )
        if step_index == STEPS - 1:
            adj_mid = adjoint
    local_sum = jnp.sum(adjoint * adjoint)
    energy = lax.psum(local_sum, "col")
    cell_count = adjoint.size * lax.axis_size("col")
    lanczos = adjoint / jnp.sqrt(energy / cell_count + eps_energy)
    return (adj_mid, lanczos)


def solution(mesh):
    in_specs = (
        P("mem", None, "col"),
        P("mem", "col", None, None),
        P("mem", "col", None),
        P("mem", None, "col"),
        P("mem", None, "col"),
    )
    out_specs = (P("mem", None, "col"), P("mem", None, "col"))
    return jax.shard_map(shards, mesh=mesh, in_specs=in_specs, out_specs=out_specs, check_vma=False)
```

profile of v0, /device:TPU:6, one launch (start us, length us, event | category | flops | bytes accessed | tf_op | source)
XLA Modules:
  0.0 414.9 jit_solution(17653825648302542761)
XLA Ops:
  0.6 0.8 slice_bitcast_fusion.4
  1.4 0.7 slice_bitcast_fusion.1
  2.2 0.7 slice_bitcast_fusion
  2.9 1.9 reshape.295
  5.3 1.5 convolution_bitcast_fusion.3
  6.9 1.7 copy.43
  8.8 47.3 %while.97 = (s32[]{:T(128)}, f32[548,8,128]{2,0,1:T(8,128)S(1)}, s32[4,4,128]{2,0,1:T(4,128)S(1)}, f32[4,4,128]{2,0,1:T(4,128)S(1)}, f32[548,4,128]{2,1,0:T(4,12...) while((s32[]{:T(128)}, f32[548,8,128]{2,0,1:T(8,128)S(1)}, ...), condition=%wide.region_4.5_spmd, body=%wide.region_0.4_spmd.sunk | while | flops 108005904 | bytes 2138801 | solution.py:61
  8.8 1.5 constant_dynamic-slice_fusion.6
  10.4 10.2 %while.100 = (s32[]{:T(128)}, f32[548,8,128]{2,0,1:T(8,128)S(1)}, s32[5]{0:T(128)S(1)}, s32[]{:T(128)}, s32[4,128]{1,0:T(4,128)S(1)}, /*index=5*/s32[4,128]{1,0:...) while((s32[]{:T(128)}, f32[548,8,128]{2,0,1:T(8,128)S(1)}, ...), condition=%wide.region_3.3_spmd, body=%wide.region_1.2_spmd.sunk | while | flops 108004368 | bytes 999768 | solution.py:44
  20.7 1.5 constant_dynamic-slice_fusion.6
  22.2 10.2 %while.100 = (s32[]{:T(128)}, f32[548,8,128]{2,0,1:T(8,128)S(1)}, s32[5]{0:T(128)S(1)}, s32[]{:T(128)}, s32[4,128]{1,0:T(4,128)S(1)}, /*index=5*/s32[4,128]{1,0:...) while((s32[]{:T(128)}, f32[548,8,128]{2,0,1:T(8,128)S(1)}, ...), condition=%wide.region_3.3_spmd, body=%wide.region_1.2_spmd.sunk | while | flops 108004368 | bytes 999768 | solution.py:44
  32.5 1.5 constant_dynamic-slice_fusion.6
  34.0 10.2 %while.100 = (s32[]{:T(128)}, f32[548,8,128]{2,0,1:T(8,128)S(1)}, s32[5]{0:T(128)S(1)}, s32[]{:T(128)}, s32[4,128]{1,0:T(4,128)S(1)}, /*index=5*/s32[4,128]{1,0:...) while((s32[]{:T(128)}, f32[548,8,128]{2,0,1:T(8,128)S(1)}, ...), condition=%wide.region_3.3_spmd, body=%wide.region_1.2_spmd.sunk | while | flops 108004368 | bytes 999768 | solution.py:44
  44.3 1.5 constant_dynamic-slice_fusion.6
  45.8 10.2 %while.100 = (s32[]{:T(128)}, f32[548,8,128]{2,0,1:T(8,128)S(1)}, s32[5]{0:T(128)S(1)}, s32[]{:T(128)}, s32[4,128]{1,0:T(4,128)S(1)}, /*index=5*/s32[4,128]{1,0:...) while((s32[]{:T(128)}, f32[548,8,128]{2,0,1:T(8,128)S(1)}, ...), condition=%wide.region_3.3_spmd, body=%wide.region_1.2_spmd.sunk | while | flops 108004368 | bytes 999768 | solution.py:44
  56.5 1.4 copy-done.2
  57.9 1.1 fusion.23
  59.0 1.9 collective-permute-start
  60.9 13.3 %collective-permute-start.1 = (f32[548,2,128]{2,1,0:T(2,128)S(1)}, f32[548,2,128]{2,1,0:T(2,128)S(1)}, u32[]{:S(2)}, u32[]{:S(2)}) collective-permute-start(f32[548,2,128]{2,1,0:T(2,128)S(1)} %get-tuple-element.1194), channel_id=1, source_target_pairs={{0,127},{1,0},{2,1},{3,2},{4,3},{5,4},{6,5},{7,6},{8,7},{9,8},{10,... | collective-permute-start | bytes 1683464 | tf_op jit(solution)/shard_map/ppermute | solution.py:19
  74.2 1.9 slice.158
  76.4 3.4 collective-permute-done
  79.8 2.3 fusion.19
  82.8 1.2 convolution_bitcast_fusion.2
  84.1 1.7 copy.51
  85.9 49.3 %while.99 = (s32[]{:T(128)}, f32[548,8,128]{2,0,1:T(8,128)S(1)}, s32[4,4,128]{2,0,1:T(4,128)S(1)}, f32[4,4,128]{2,0,1:T(4,128)S(1)}, f32[548,4,128]{2,1,0:T(4,12...) while((s32[]{:T(128)}, f32[548,8,128]{2,0,1:T(8,128)S(1)}, ...), condition=%wide.region_9.10_spmd, body=%wide.region_5.9_spmd.sunk | while | flops 108005904 | bytes 2138801 | solution.py:61
  86.0 1.5 constant_dynamic-slice_fusion.7
  87.6 10.7 %while.101 = (s32[]{:T(128)}, f32[548,8,128]{2,0,1:T(8,128)S(1)}, s32[5]{0:T(128)S(1)}, s32[]{:T(128)}, s32[4,128]{1,0:T(4,128)S(1)}, /*index=5*/s32[4,128]{1,0:...) while((s32[]{:T(128)}, f32[548,8,128]{2,0,1:T(8,128)S(1)}, ...), condition=%wide.region_8.8_spmd, body=%wide.region_6.7_spmd.sunk | while | flops 108004368 | bytes 999768 | solution.py:44
  89.7 0.6 dynamic_slice.173
  94.0 0.6 dynamic_slice.173
  96.1 0.6 dynamic_slice.173
  98.3 1.5 constant_dynamic-slice_fusion.7
  99.9 10.7 %while.101 = (s32[]{:T(128)}, f32[548,8,128]{2,0,1:T(8,128)S(1)}, s32[5]{0:T(128)S(1)}, s32[]{:T(128)}, s32[4,128]{1,0:T(4,128)S(1)}, /*index=5*/s32[4,128]{1,0:...) while((s32[]{:T(128)}, f32[548,8,128]{2,0,1:T(8,128)S(1)}, ...), condition=%wide.region_8.8_spmd, body=%wide.region_6.7_spmd.sunk | while | flops 108004368 | bytes 999768 | solution.py:44
  110.7 1.5 constant_dynamic-slice_fusion.7
  112.2 10.7 %while.101 = (s32[]{:T(128)}, f32[548,8,128]{2,0,1:T(8,128)S(1)}, s32[5]{0:T(128)S(1)}, s32[]{:T(128)}, s32[4,128]{1,0:T(4,128)S(1)}, /*index=5*/s32[4,128]{1,0:...) while((s32[]{:T(128)}, f32[548,8,128]{2,0,1:T(8,128)S(1)}, ...), condition=%wide.region_8.8_spmd, body=%wide.region_6.7_spmd.sunk | while | flops 108004368 | bytes 999768 | solution.py:44
  123.0 1.5 constant_dynamic-slice_fusion.7
  124.5 10.7 %while.101 = (s32[]{:T(128)}, f32[548,8,128]{2,0,1:T(8,128)S(1)}, s32[5]{0:T(128)S(1)}, s32[]{:T(128)}, s32[4,128]{1,0:T(4,128)S(1)}, /*index=5*/s32[4,128]{1,0:...) while((s32[]{:T(128)}, f32[548,8,128]{2,0,1:T(8,128)S(1)}, ...), condition=%wide.region_8.8_spmd, body=%wide.region_6.7_spmd.sunk | while | flops 108004368 | bytes 999768 | solution.py:44
  135.7 1.4 copy-done.3
  137.0 1.3 fusion.22
  138.4 2.0 collective-permute-start.2
  140.4 7.1 %collective-permute-start.3 = (f32[548,2,128]{2,1,0:T(2,128)}, f32[548,2,128]{2,1,0:T(2,128)}, u32[]{:S(2)}, u32[]{:S(2)}) collective-permute-start(f32[548,2,128]{2,1,0:T(2,128)} %get-tuple-element.1192), channel_id=1, source_target_pairs={{0,127},{1,0},{2,1},{3,2},{4,3},{5,4},{6,5},{7,6},{8,7},{9,8},{10,... | collective-permute-start | bytes 1683464 | tf_op jit(solution)/shard_map/ppermute | solution.py:19
  147.6 1.5 reshape.297
  149.3 3.7 collective-permute-done.2
  153.0 1.7 fusion.17
  154.8 1.7 fusion.16
  156.5 1.2 multiply_reduce_fusion
  157.7 1.7 copy.57
  159.4 252.6 %psum.7 = f32[]{:T(128)} all-reduce(f32[]{:T(128)} %multiply_reduce_fusion), channel_id=1, replica_groups=mesh['mem'=4,'col'=128] {'col'}, use_global_device_ids=true, to_apply=%region_11.12 | all-reduce | flops 1 | bytes 8 | tf_op jit(solution)/shard_map/psum | solution.py:105
  413.2 1.7 copy.58
  (262 shorter events, 59.3 us)
Async XLA Ops:
  0.6 4.2 %copy-start.6 = (f32[2,4,137,137]{3,1,2,0:T(4,128)S(1)}, f32[2,4,137,137]{3,1,2,0:T(4,128)}, u32[]{:S(2)}) copy-start(f32[2,4,137,137]{3,1,2,0:T(4,128)} %param.22) | copy-start | bytes 1801828
  56.5 1.4 copy-start.2
  59.0 20.8 %collective-permute-start = (f32[548,2,128]{2,1,0:T(2,128)}, f32[548,2,128]{2,1,0:T(2,128)}, u32[]{:S(2)}, u32[]{:S(2)}) collective-permute-start(f32[548,2,128]{2,1,0:T(2,128)} %get-tuple-element.1195), channel_id=1, source_target_pairs={{0,1},{1,2},{2,3},{3,4},{4,5},{5,6},{6,7},{7,8},{8,9},{9,10},{10,1... | collective-permute-start | bytes 1683464 | tf_op jit(solution)/shard_map/ppermute | solution.py:19
  60.9 21.3 %collective-permute-start.1 = (f32[548,2,128]{2,1,0:T(2,128)S(1)}, f32[548,2,128]{2,1,0:T(2,128)S(1)}, u32[]{:S(2)}, u32[]{:S(2)}) collective-permute-start(f32[548,2,128]{2,1,0:T(2,128)S(1)} %get-tuple-element.1194), channel_id=1, source_target_pairs={{0,127},{1,0},{2,1},{3,2},{4,3},{5,4},{6,5},{7,6},{8,7},{9,8},{10,... | collective-permute-start | bytes 1683464 | tf_op jit(solution)/shard_map/ppermute | solution.py:19
  82.8 1.2 copy-start
  135.7 1.4 copy-start.3
  137.0 10.5 %copy-start.1 = (f32[548,4,128]{2,1,0:T(4,128)S(1)}, f32[548,4,128]{2,1,0:T(4,128)}, u32[]{:S(2)}) copy-start(f32[548,4,128]{2,1,0:T(4,128)} %copy-done) | copy-start | bytes 3366916
  138.4 10.7 %copy-start.4 = (f32[548,8,128]{2,1,0:T(8,128)S(1)}, f32[548,8,128]{2,1,0:T(8,128)}, u32[]{:S(2)}) copy-start(f32[548,8,128]{2,1,0:T(8,128)} %copy-done.3) | copy-start | bytes 6733828
  138.4 14.7 %collective-permute-start.2 = (f32[548,2,128]{2,1,0:T(2,128)}, f32[548,2,128]{2,1,0:T(2,128)}, u32[]{:S(2)}, u32[]{:S(2)}) collective-permute-start(f32[548,2,128]{2,1,0:T(2,128)} %get-tuple-element.1193), channel_id=1, source_target_pairs={{0,1},{1,2},{2,3},{3,4},{4,5},{5,6},{6,7},{7,8},{8,9},{9,10},{10,1... | collective-permute-start | bytes 1683464 | tf_op jit(solution)/shard_map/ppermute | solution.py:19
  140.4 14.4 %collective-permute-start.3 = (f32[548,2,128]{2,1,0:T(2,128)}, f32[548,2,128]{2,1,0:T(2,128)}, u32[]{:S(2)}, u32[]{:S(2)}) collective-permute-start(f32[548,2,128]{2,1,0:T(2,128)} %get-tuple-element.1192), channel_id=1, source_target_pairs={{0,127},{1,0},{2,1},{3,2},{4,3},{5,4},{6,5},{7,6},{8,7},{9,8},{10,... | collective-permute-start | bytes 1683464 | tf_op jit(solution)/shard_map/ppermute | solution.py:19
  154.7 3.0 copy-start.5
where the time goes:
time: 416 us; the launch traced here: 415 us
  blocking collectives  253 us (61%)
  local copies, waits for them, and re-layouts  58.9 us (14%)
  matrix products  26.9 us (6%)
  loops' own time  26.9 us (6%)
  starting transfers between devices  24.4 us (6%)
  other arithmetic  16.5 us (4%)
  waiting for transfers between devices  7.24 us (2%)
    psum x1, blocking collectives, shards(): energy = lax.psum(local_sum, 'col')  253 us
    another operation x8, loops' own time, add_block(): return lax.fori_loop(0, slot_limit, one_slot, accumulated)  26.4 us
    ppermute x4, starting transfers between devices, passed_along(): return lax.ppermute(value, axis, pairs)  24.4 us
    dynamic_slice x40, local copies, waits for them, and re-layouts, one_slot(): position, inside = locate(route_row[slot_number])  24.3 us
    dot_general x40, matrix products, one_slot(): jnp.dot(block_rows, matrix, precision=lax.Precision.HIGHEST, preferred_el...  24.1 us
    dynamic_slice x16, local copies, waits for them, and re-layouts, one_block(): lax.dynamic_index_in_dim(rows_all, block_index, 1, keepdims=False)  12.2 us
  transfers between devices with their start and end apart: 4, of which 3 were waited for; matrix products, arithmetic and copies ran while one was open for 2% of the time, Pallas kernels for 0%

commit v1 on v0

v1 whole, which is shorter than its diff:
```python
import functools

import jax
import jax.numpy as jnp
from jax import lax
from jax.experimental import pallas as pl
from jax.experimental.pallas import tpu as pltpu
from jax.sharding import PartitionSpec as P

BCOLS = 128
REACH = 2
SLOTS = 5
POINTS = 4
STEPS = 2
PAIR = 2 * BCOLS
WINDOW = 3 * PAIR
EPS_ENERGY = 1e-06
GROUP = 8
CHUNKS = 2
MESH = pl.DeviceIdType.MESH
F32 = jnp.float32
BF16 = jnp.bfloat16


def halves(value):
    high = value.astype(BF16)
    low = (value - high.astype(F32)).astype(BF16)
    return high, low


def kernel(
    count,
    lists_hbm,
    points_hbm,
    weights_hbm,
    adj_hbm,
    inv_hbm,
    mid_ref,
    out_ref,
    lists_ref,
    points_ref,
    weights_ref,
    adj_in,
    inv_in,
    adj_pad,
    inv_pad,
    w_high,
    w_low,
    own,
    send_buf,
    recv_buf,
    near_buf,
    far_buf,
    small_sem,
    in_sem,
    inv_sem,
    send_sem,
    recv_sem,
    near_send,
    near_recv,
    far_send,
    far_recv,
):
    variables, padded, col_count = adj_pad.shape
    levels = inv_in.shape[-1]
    blocks = col_count // BCOLS
    pairs = blocks // 2
    tiles = pairs + 2
    per_chunk = variables // CHUNKS
    all_blocks = count * blocks
    me = lax.axis_index("col")
    up = lax.rem(me + 1, count)
    down = lax.rem(me + count - 1, count)
    group = min(GROUP, count)
    far_count = count // group
    near_me = lax.rem(me, group)
    far_me = me // group
    near_peers = [far_me * group + lax.rem(near_me + j, group) for j in range(1, group)]
    far_peers = [lax.rem(far_me + j, far_count) * group + near_me for j in range(1, far_count)]

    barrier = pltpu.get_barrier_semaphore()
    everyone = [up, down] + near_peers + far_peers
    for peer in everyone:
        pl.semaphore_signal(barrier, inc=1, device_id={"col": peer}, device_id_type=MESH)

    small_copies = [
        pltpu.make_async_copy(lists_hbm, lists_ref, small_sem.at[0]),
        pltpu.make_async_copy(points_hbm, points_ref, small_sem.at[1]),
        pltpu.make_async_copy(weights_hbm, weights_ref, small_sem.at[2]),
    ]
    inv_copies = {
        step: [
            pltpu.make_async_copy(
                inv_hbm.at[step, :, source, :], inv_in.at[step, source], inv_sem.at[step, source]
            )
            for source in range(blocks)
        ]
        for step in range(STEPS)
    }
    adj_copy = pltpu.make_async_copy(adj_hbm, adj_in, in_sem.at[0])
    for copy in small_copies + inv_copies[1] + [adj_copy] + inv_copies[0]:
        copy.start()

    whole = levels // 8 * 8
    stride = variables * blocks

    def pieces(v, source):
        first = source * variables + v
        yield slice(0, whole), pl.ds(first, whole, stride=stride)
        for level in range(whole, levels):
            yield slice(level, level + 1), pl.ds(level * stride + first, 1)

    def build(step):
        points = points_ref[step]
        slot_ids = points // BCOLS
        within = points % BCOLS
        for source in range(blocks):
            lanes = slice(source * BCOLS, (source + 1) * BCOLS)
            block = me * blocks + source
            slots = slot_ids[:, lanes]
            offset = jnp.zeros_like(slots)
            for slot in range(SLOTS):
                rel = lists_ref[step, source, slot] - block + REACH
                rel = jnp.where(rel < 0, rel + all_blocks, rel)
                rel = jnp.where(rel >= all_blocks, rel - all_blocks, rel)
                offset = jnp.where(slots == slot, rel, offset)
            column = offset * BCOLS + within[:, lanes]
            weight = weights_ref[step][:, lanes]
            parity = source % 2
            pair = source // 2
            half = slice(parity * BCOLS, (parity + 1) * BCOLS)
            empty = jnp.zeros((BCOLS, BCOLS), BF16)
            unused = slice(0, BCOLS) if parity else slice(SLOTS * BCOLS, WINDOW)
            w_high[step, pair, unused, half] = empty
            w_low[step, pair, unused, half] = empty
            for piece in range(SLOTS):
                rows = lax.broadcasted_iota(jnp.int32, (BCOLS, BCOLS), 0) + piece * BCOLS
                total = jnp.zeros((BCOLS, BCOLS), F32)
                for point in range(POINTS):
                    hit = rows == column[point : point + 1]
                    total = total + jnp.where(hit, weight[point : point + 1], 0.0)
                high, low = halves(total)
                place = slice((piece + parity) * BCOLS, (piece + parity + 1) * BCOLS)
                w_high[step, pair, place, half] = high
                w_low[step, pair, place, half] = low

    def pad_inverse(step):
        for source in range(blocks):
            inv_pad[source] = jnp.zeros((padded, padded), F32)
            inv_pad[source, 0:levels, 0:levels] = inv_in[step, source]

    def stacked_inverse(source):
        high, low = halves(inv_pad[source])
        return jnp.concatenate([high, low, high], axis=0)

    def diffuse(inverse, value):
        high, low = halves(value)
        return lax.dot_general(
            inverse,
            jnp.concatenate([high, high, low], axis=0),
            (((0,), (0,)), ((), ())),
            preferred_element_type=F32,
        )

    def diffused_pairs(block_value, inverses):
        result = []
        for pair in range(pairs):
            left = diffuse(inverses[2 * pair], block_value(2 * pair))
            right = diffuse(inverses[2 * pair + 1], block_value(2 * pair + 1))
            rows = [
                jnp.concatenate(
                    [left[:, v * BCOLS : (v + 1) * BCOLS], right[:, v * BCOLS : (v + 1) * BCOLS]], axis=1
                )
                for v in range(per_chunk)
            ]
            result.append(halves(jnp.concatenate(rows, axis=0)))
        return result

    def tile_sum(step, diffused, tile):
        left, right = [], []
        for pair in range(pairs):
            if 0 <= tile - pair <= 2:
                high, low = diffused[pair]
                place = slice((tile - pair) * PAIR, (tile - pair + 1) * PAIR)
                left += [high, low, high]
                matrix = w_high[step, pair, place, :]
                right += [matrix, matrix, w_low[step, pair, place, :]]
        return lax.dot_general(
            jnp.concatenate(left, axis=1),
            jnp.concatenate(right, axis=1),
            (((1,), (1,)), ((), ())),
            preferred_element_type=F32,
        )

    def halo_copy(exchange, chunk, way):
        return pltpu.make_async_remote_copy(
            src_ref=send_buf.at[exchange, chunk, way],
            dst_ref=recv_buf.at[exchange, chunk, way],
            send_sem=send_sem.at[exchange, chunk, way],
            recv_sem=recv_sem.at[exchange, chunk, way],
            device_id={"col": up if way else down},
            device_id_type=MESH,
        )

    def scatter(exchange, step, chunk, diffused, first):
        for way, tile in ((0, 0), (1, tiles - 1)):
            value = tile_sum(step, diffused, tile)
            for v in range(per_chunk):
                send_buf[exchange, chunk, way, v] = value[v * padded : (v + 1) * padded]
        if first:
            pl.semaphore_wait(barrier, len(everyone))
        for way in range(2):
            halo_copy(exchange, chunk, way).start()
        for tile in range(1, tiles - 1):
            value = tile_sum(step, diffused, tile)
            for v in range(per_chunk):
                own[chunk * per_chunk + v, :, (tile - 1) * PAIR : tile * PAIR] = value[
                    v * padded : (v + 1) * padded
                ]

    def arrived(exchange, chunk):
        for way in range(2):
            halo_copy(exchange, chunk, way).wait_recv()
        for v in range(per_chunk):
            row = chunk * per_chunk + v
            own[row, :, 0:PAIR] = own[row, :, 0:PAIR] + recv_buf[exchange, chunk, 1, v]
            last = slice(col_count - PAIR, col_count)
            own[row, :, last] = own[row, :, last] + recv_buf[exchange, chunk, 0, v]

    for copy in small_copies:
        copy.wait()
    build(1)
    for copy in inv_copies[1]:
        copy.wait()
    pad_inverse(1)
    inverses = [stacked_inverse(source) for source in range(blocks)]
    for v in range(variables):
        adj_pad[v, padded - 8 : padded, :] = jnp.zeros((8, col_count), F32)
    for chunk in range(CHUNKS):
        if chunk == 0:
            adj_copy.wait()
        for v in range(chunk * per_chunk, (chunk + 1) * per_chunk):
            for source in range(blocks):
                lanes = slice(source * BCOLS, (source + 1) * BCOLS)
                for part, rows in pieces(v, source):
                    adj_pad[v, part, lanes] = adj_in[rows, :]

        def block_value(source, chunk=chunk):
            lanes = slice(source * BCOLS, (source + 1) * BCOLS)
            return jnp.concatenate(
                [adj_pad[v, :, lanes] for v in range(chunk * per_chunk, (chunk + 1) * per_chunk)], axis=1
            )

        scatter(0, 1, chunk, diffused_pairs(block_value, inverses), chunk == 0)

    build(0)
    for copy in inv_copies[0]:
        copy.wait()
    pad_inverse(0)
    inverses = [stacked_inverse(source) for source in range(blocks)]
    for chunk in range(CHUNKS):
        arrived(0, chunk)
        for v in range(chunk * per_chunk, (chunk + 1) * per_chunk):
            for source in range(blocks):
                for part, rows in pieces(v, source):
                    mid_ref[rows, :] = own[v, part, source * BCOLS : (source + 1) * BCOLS]

        def block_value(source, chunk=chunk):
            lanes = slice(source * BCOLS, (source + 1) * BCOLS)
            return jnp.concatenate(
                [own[v, :, lanes] for v in range(chunk * per_chunk, (chunk + 1) * per_chunk)], axis=1
            )

        scatter(1, 0, chunk, diffused_pairs(block_value, inverses), False)

    total = jnp.zeros((8, BCOLS), F32)
    for chunk in range(CHUNKS):
        arrived(1, chunk)
        for v in range(chunk * per_chunk, (chunk + 1) * per_chunk):
            value = own[v]
            square = value * value
            by_lane = square[:, 0:BCOLS]
            for block in range(1, blocks):
                by_lane = by_lane + square[:, block * BCOLS : (block + 1) * BCOLS]
            total = total + jnp.sum(by_lane.reshape(padded // 8, 8, BCOLS), axis=0)

    near_buf[near_me] = total
    near_copies = [
        pltpu.make_async_remote_copy(
            src_ref=near_buf.at[near_me],
            dst_ref=near_buf.at[near_me],
            send_sem=near_send.at[j],
            recv_sem=near_recv.at[near_me],
            device_id={"col": peer},
            device_id_type=MESH,
        )
        for j, peer in enumerate(near_peers)
    ]
    for copy in near_copies:
        copy.start()
    for j, peer in enumerate(near_peers):
        slot = lax.rem(near_me + j + 1, group)
        pltpu.make_async_remote_copy(
            src_ref=near_buf.at[slot],
            dst_ref=near_buf.at[slot],
            send_sem=near_send.at[j],
            recv_sem=near_recv.at[slot],
            device_id={"col": peer},
            device_id_type=MESH,
        ).wait_recv()
    total = near_buf[0]
    for slot in range(1, group):
        total = total + near_buf[slot]
    far_buf[far_me] = total
    far_copies = [
        pltpu.make_async_remote_copy(
            src_ref=far_buf.at[far_me],
            dst_ref=far_buf.at[far_me],
            send_sem=far_send.at[j],
            recv_sem=far_recv.at[far_me],
            device_id={"col": peer},
            device_id_type=MESH,
        )
        for j, peer in enumerate(far_peers)
    ]
    for copy in far_copies:
        copy.start()
    for j, peer in enumerate(far_peers):
        slot = lax.rem(far_me + j + 1, far_count)
        pltpu.make_async_remote_copy(
            src_ref=far_buf.at[slot],
            dst_ref=far_buf.at[slot],
            send_sem=far_send.at[j],
            recv_sem=far_recv.at[slot],
            device_id={"col": peer},
            device_id_type=MESH,
        ).wait_recv()
    total = far_buf[0]
    for slot in range(1, far_count):
        total = total + far_buf[slot]
    energy = jnp.sum(jnp.sum(total, axis=1, keepdims=True), axis=0, keepdims=True)
    cells = variables * levels * col_count * count
    root = jnp.sqrt(energy / cells + EPS_ENERGY)
    scale = 1.0 / root
    for v in range(variables):
        for source in range(blocks):
            for part, rows in pieces(v, source):
                out_ref[rows, :] = own[v, part, source * BCOLS : (source + 1) * BCOLS] * scale
    for exchange in range(2):
        for chunk in range(CHUNKS):
            for way in range(2):
                halo_copy(exchange, chunk, way).wait_send()
    for copy in near_copies + far_copies:
        copy.wait_send()


def shards(adj_final, inverses, dep_lists, dep_points, weights):
    variables, levels, col_count = adj_final.shape
    count = lax.axis_size("col")
    blocks = col_count // BCOLS
    padded = -(-levels // 16) * 16
    pairs = blocks // 2
    per_chunk = variables // CHUNKS
    group = min(GROUP, count)
    far_count = count // group
    halo = (2, CHUNKS, 2, per_chunk, padded, PAIR)
    rows = levels * blocks * variables
    like = jax.ShapeDtypeStruct((rows, BCOLS), F32)
    adj_rows = adj_final.reshape(variables, levels, blocks, BCOLS).transpose(1, 2, 0, 3).reshape(rows, BCOLS)
    outs = pl.pallas_call(
        functools.partial(kernel, count),
        out_shape=(like, like),
        in_specs=[pl.BlockSpec(memory_space=pltpu.HBM)] * 5,
        out_specs=(pl.BlockSpec(memory_space=pltpu.VMEM), pl.BlockSpec(memory_space=pltpu.VMEM)),
        scratch_shapes=[
            pltpu.SMEM(dep_lists.shape, jnp.int32),
            pltpu.VMEM(dep_points.shape, jnp.int32),
            pltpu.VMEM(weights.shape, F32),
            pltpu.VMEM((rows, BCOLS), F32),
            pltpu.VMEM((STEPS, blocks, levels, levels), F32),
            pltpu.VMEM((variables, padded, col_count), F32),
            pltpu.VMEM((blocks, padded, padded), F32),
            pltpu.VMEM((STEPS, pairs, WINDOW, PAIR), BF16),
            pltpu.VMEM((STEPS, pairs, WINDOW, PAIR), BF16),
            pltpu.VMEM((variables, padded, col_count), F32),
            pltpu.VMEM(halo, F32),
            pltpu.VMEM(halo, F32),
            pltpu.VMEM((group, 8, BCOLS), F32),
            pltpu.VMEM((far_count, 8, BCOLS), F32),
            pltpu.SemaphoreType.DMA((3,)),
            pltpu.SemaphoreType.DMA((1,)),
            pltpu.SemaphoreType.DMA((STEPS, blocks)),
            pltpu.SemaphoreType.DMA((2, CHUNKS, 2)),
            pltpu.SemaphoreType.DMA((2, CHUNKS, 2)),
            pltpu.SemaphoreType.DMA((group,)),
            pltpu.SemaphoreType.DMA((group,)),
            pltpu.SemaphoreType.DMA((far_count,)),
            pltpu.SemaphoreType.DMA((far_count,)),
        ],
        compiler_params=pltpu.CompilerParams(
            collective_id=0, has_side_effects=True, vmem_limit_bytes=64 << 20
        ),
    )(dep_lists, dep_points, weights, adj_rows, inverses.transpose(0, 2, 1, 3))
    return tuple(
        out.reshape(levels, blocks, variables, BCOLS).transpose(2, 0, 1, 3).reshape(adj_final.shape)
        for out in outs
    )


def solution(mesh):
    in_specs = (
        P("mem", None, "col"),
        P("mem", "col", None, None),
        P("mem", "col", None),
        P("mem", None, "col"),
        P("mem", None, "col"),
    )
    out_specs = (P("mem", None, "col"), P("mem", None, "col"))
    return jax.shard_map(shards, mesh=mesh, in_specs=in_specs, out_specs=out_specs, check_vma=False)
```

time: 416 us -> 49.5 us (0.12)
  blocking collectives: 253 us -> 0 us
  local copies, waits for them, and re-layouts: 58.9 us -> 3.53 us
  Pallas kernels: 0 us -> 44.8 us
  matrix products: 26.9 us -> 0 us
  loops' own time: 26.9 us -> 0 us
  starting transfers between devices: 24.4 us -> 0 us
  other arithmetic: 16.5 us -> 0 us
  waiting for transfers between devices: 7.24 us -> 0 us
    psum x1 -> x0, blocking collectives: 253 us -> none  [shards(): energy = lax.psum(local_sum, 'col')]
    pallas_call x0 -> x1, Pallas kernels: none -> 44.8 us  [shards(): pl.pallas_call(functools.partial(kernel, count), out_shape=(like, like),...]
    dynamic_slice x56 -> x0, local copies, waits for them, and re-layouts: 36.4 us -> none  [the longest x40 24.3 us: one_slot(): position, inside = locate(route_row[slot_number])]
    another operation x10 -> x0, loops' own time: 26.9 us -> none  [the longest x8 26.4 us: add_block(): return lax.fori_loop(0, slot_limit, one_slot, accumulated)]
    dot_general x42 -> x0, matrix products: 26.9 us -> none  [the longest x40 24.1 us: one_slot(): jnp.dot(block_rows, matrix, precision=lax.Precision.HIGHEST, preferred_el...]
    ppermute x4 -> x0, starting transfers between devices: 24.4 us -> none  [passed_along(): return lax.ppermute(value, axis, pairs)]
    reduce_sum x41 -> x0, other arithmetic: 9.18 us -> none  [the longest x40 8 us: slot_matrix(): return jnp.sum(one_hot * chosen[:, :, None], axis=0)]
    ppermute x4 -> x0, waiting for transfers between devices: 7.24 us -> none  [passed_along(): return lax.ppermute(value, axis, pairs)]
  transfers between devices with their start and end apart: 4 -> 0, of which waited for: 3 -> 0; matrix products, arithmetic and copies ran while one was open for 2% -> 0% of each run, Pallas kernels for 0% -> 0%
where the time goes in v1:
time: 49.5 us; the launch traced here: 49 us
  Pallas kernels  44.8 us (91%)
  local copies, waits for them, and re-layouts  3.53 us (7%)
  between operations  0.65 us (1%)
    pallas_call x1, Pallas kernels, shards(): pl.pallas_call(functools.partial(kernel, count), out_shape=(like, like),...  44.8 us
    unnamed x4, local copies, waits for them, and re-layouts  3.53 us

profile of v1, /device:TPU:6, one launch (start us, length us, event | category | flops | bytes accessed | tf_op | source)
XLA Modules:
  0.0 49.0 jit_solution(11106690383486273589)
XLA Ops:
  0.6 44.8 %shard_map.68 = (f32[2192,128]{1,0:T(8,128)}, f32[2192,128]{1,0:T(8,128)}) custom-call(s32[2,4,5]{2,1,0:T(4,128)} %lists_hbm.1, s32[2,4,512]{2,1,0:T(4,128)} %points_hbm.1, f32[2,4,512]{2,1,0:T(4,128)} %weights_hbm.1, f32[2192,128]{1,0:T(8,128)} %bitcast.16, f32[2,137,4,137]{3,2,1,0:T(4,128)} %bitcast.17), custom_call_target="tpu_custom_call" | custom-call | tf_op jit(solution)/shard_map/pallas_call | solution.py:370
  45.5 0.0 copy-start
  45.5 2.5 %copy.12 = f32[4,137,512]{2,0,1:T(4,128)} copy(f32[4,137,512]{2,0,1:T(4,128)} %bitcast.19) | data formatting | bytes 2244608
  48.0 0.0 copy-done
  48.0 1.0 %copy.13 = f32[4,137,512]{2,0,1:T(4,128)} copy(f32[4,137,512]{2,0,1:T(4,128)S(1)} %bitcast.18) | data formatting | bytes 2244608
Async XLA Ops:
  45.5 2.5 %copy-start = (f32[2192,128]{1,0:T(8,128)S(1)}, f32[2192,128]{1,0:T(8,128)}, u32[]{:S(2)}) copy-start(f32[2192,128]{1,0:T(8,128)} %get-tuple-element.5) | copy-start | bytes 3366916

commit v2 on v1

--- a/solution.py
+++ b/solution.py
@@ -16,7 +16,7 @@
 WINDOW = 3 * PAIR
 EPS_ENERGY = 1e-06
 GROUP = 8
-CHUNKS = 2
+CHUNKS = 4
 MESH = pl.DeviceIdType.MESH
 F32 = jnp.float32
 BF16 = jnp.bfloat16
@@ -36,7 +36,8 @@
     adj_hbm,
     inv_hbm,
     mid_ref,
-    out_ref,
+    start_ref,
+    energy_ref,
     lists_ref,
     points_ref,
     weights_ref,
@@ -283,6 +284,7 @@
             for block in range(1, blocks):
                 by_lane = by_lane + square[:, block * BCOLS : (block + 1) * BCOLS]
             total = total + jnp.sum(by_lane.reshape(padded // 8, 8, BCOLS), axis=0)
+    total = jnp.sum(total, axis=0, keepdims=True)
 
     near_buf[near_me] = total
     near_copies = [
@@ -298,6 +300,10 @@
     ]
     for copy in near_copies:
         copy.start()
+    for v in range(variables):
+        for source in range(blocks):
+            for part, rows in pieces(v, source):
+                start_ref[rows, :] = own[v, part, source * BCOLS : (source + 1) * BCOLS]
     for j, peer in enumerate(near_peers):
         slot = lax.rem(near_me + j + 1, group)
         pltpu.make_async_remote_copy(
@@ -338,20 +344,25 @@
     total = far_buf[0]
     for slot in range(1, far_count):
         total = total + far_buf[slot]
-    energy = jnp.sum(jnp.sum(total, axis=1, keepdims=True), axis=0, keepdims=True)
-    cells = variables * levels * col_count * count
-    root = jnp.sqrt(energy / cells + EPS_ENERGY)
-    scale = 1.0 / root
-    for v in range(variables):
-        for source in range(blocks):
-            for part, rows in pieces(v, source):
-                out_ref[rows, :] = own[v, part, source * BCOLS : (source + 1) * BCOLS] * scale
+    energy_ref[...] = total
     for exchange in range(2):
         for chunk in range(CHUNKS):
             for way in range(2):
                 halo_copy(exchange, chunk, way).wait_send()
     for copy in near_copies + far_copies:
         copy.wait_send()
+
+
+def finish(cells, mid_in, start_in, energy_ref, mid_hbm, out_hbm, scaled, sem):
+    mid_copy = pltpu.make_async_copy(mid_in, mid_hbm, sem.at[0])
+    mid_copy.start()
+    energy = jnp.sum(energy_ref[...], axis=1, keepdims=True)
+    scale = 1.0 / jnp.sqrt(energy / cells + EPS_ENERGY)
+    scaled[...] = start_in[...] * scale
+    out_copy = pltpu.make_async_copy(scaled, out_hbm, sem.at[1])
+    out_copy.start()
+    mid_copy.wait()
+    out_copy.wait()
 
 
 def shards(adj_final, inverses, dep_lists, dep_points, weights):
@@ -367,11 +378,13 @@
     rows = levels * blocks * variables
     like = jax.ShapeDtypeStruct((rows, BCOLS), F32)
     adj_rows = adj_final.reshape(variables, levels, blocks, BCOLS).transpose(1, 2, 0, 3).reshape(rows, BCOLS)
-    outs = pl.pallas_call(
+    vmem = pl.BlockSpec(memory_space=pltpu.VMEM)
+    anywhere = pl.BlockSpec(memory_space=pltpu.HBM)
+    mid, start, energy = pl.pallas_call(
         functools.partial(kernel, count),
-        out_shape=(like, like),
+        out_shape=(like, like, jax.ShapeDtypeStruct((1, BCOLS), F32)),
         in_specs=[pl.BlockSpec(memory_space=pltpu.HBM)] * 5,
-        out_specs=(pl.BlockSpec(memory_space=pltpu.VMEM), pl.BlockSpec(memory_space=pltpu.VMEM)),
+        out_specs=(vmem, vmem, vmem),
         scratch_shapes=[
             pltpu.SMEM(dep_lists.shape, jnp.int32),
             pltpu.VMEM(dep_points.shape, jnp.int32),
@@ -385,8 +398,8 @@
             pltpu.VMEM((variables, padded, col_count), F32),
             pltpu.VMEM(halo, F32),
             pltpu.VMEM(halo, F32),
-            pltpu.VMEM((group, 8, BCOLS), F32),
-            pltpu.VMEM((far_count, 8, BCOLS), F32),
+            pltpu.VMEM((group, 1, BCOLS), F32),
+            pltpu.VMEM((far_count, 1, BCOLS), F32),
             pltpu.SemaphoreType.DMA((3,)),
             pltpu.SemaphoreType.DMA((1,)),
             pltpu.SemaphoreType.DMA((STEPS, blocks)),
@@ -398,9 +411,22 @@
             pltpu.SemaphoreType.DMA((far_count,)),
         ],
         compiler_params=pltpu.CompilerParams(
-            collective_id=0, has_side_effects=True, vmem_limit_bytes=64 << 20
+            collective_id=0, has_side_effects=True, vmem_limit_bytes=48 << 20
         ),
-    )(dep_lists, dep_points, weights, adj_rows, inverses.transpose(0, 2, 1, 3))
+    )(
+        *(
+            pltpu.with_memory_space_constraint(value, pltpu.HBM)
+            for value in (dep_lists, dep_points, weights, adj_rows, inverses.transpose(0, 2, 1, 3))
+        )
+    )
+    outs = pl.pallas_call(
+        functools.partial(finish, count * adj_final.size),
+        out_shape=(like, like),
+        in_specs=[vmem, vmem, vmem],
+        out_specs=(anywhere, anywhere),
+        scratch_shapes=[pltpu.VMEM((rows, BCOLS), F32), pltpu.SemaphoreType.DMA((2,))],
+        compiler_params=pltpu.CompilerParams(vmem_limit_bytes=16 << 20),
+    )(mid, start, energy)
     return tuple(
         out.reshape(levels, blocks, variables, BCOLS).transpose(2, 0, 1, 3).reshape(adj_final.shape)
         for out in outs

time: 49.5 us -> 43.3 us (0.87)
  local copies, waits for them, and re-layouts: 3.53 us -> 0 us
  Pallas kernels: 44.8 us -> 42 us
    unnamed x4 -> x0, local copies, waits for them, and re-layouts: 3.53 us -> none
    pallas_call x1 -> x2, Pallas kernels: 44.8 us -> 42 us  [the longest x1 40.6 us: shards(): pl.pallas_call(functools.partial(kernel, count), out_shape=(like, like, j...]
where the time goes in v2:
time: 43.3 us; the launch traced here: 42.6 us
  Pallas kernels  42 us (97%)
  between operations  0.64 us (1%)
    pallas_call x1, Pallas kernels, shards(): pl.pallas_call(functools.partial(kernel, count), out_shape=(like, like, j...  40.6 us
    pallas_call x1, Pallas kernels, shards(): pl.pallas_call(functools.partial(finish, count * adj_final.size), out_sha...  1.38 us

profile of v2, /device:TPU:6, one launch (start us, length us, event | category | flops | bytes accessed | tf_op | source)
XLA Modules:
  0.0 42.6 jit_solution(4078717095624496268)
XLA Ops:
  0.6 40.6 %shard_map.68 = (f32[2192,128]{1,0:T(8,128)S(1)}, f32[2192,128]{1,0:T(8,128)S(1)}, f32[1,128]{1,0:T(1,128)S(1)}) custom-call(s32[2,4,5]{2,1,0:T(4,128)} %lists_hbm.1, s32[2,4,512]{2,1,0:T(4,128)} %points_hbm.1, f32[2,4,512]{2,1,0:T(4,128)} %weights_hbm.1, f32[2192,128]{1,0:T(8,128)} %bitcast.16, f32[2,137,4,137]{3,2,1,0:T(4,128)} %bitcast.17), custom_call_target="tpu_custom_call" | custom-call | tf_op jit(solution)/shard_map/pallas_call | solution.py:383
  41.3 1.4 %shard_map.69 = (f32[2192,128]{1,0:T(8,128)}, f32[2192,128]{1,0:T(8,128)}) custom-call(f32[2192,128]{1,0:T(8,128)S(1)} %get-tuple-element.7.mid_in, f32[2192,128]{1,0:T(8,128)S(1)} %get-tuple-element.8.start_in, f32[1,128]{1,0:T(1,128)S(1)} %get-tuple-element.9.energy_ref), custom_call_target="tpu_custom_call" | custom-call | tf_op jit(solution)/shard_map/pallas_call | solution.py:422

commit v3 on v2

--- a/solution.py
+++ b/solution.py
@@ -52,6 +52,7 @@
     recv_buf,
     near_buf,
     far_buf,
+    line_sem,
     small_sem,
     in_sem,
     inv_sem,
@@ -76,12 +77,20 @@
     far_count = count // group
     near_me = lax.rem(me, group)
     far_me = me // group
-    near_peers = [far_me * group + lax.rem(near_me + j, group) for j in range(1, group)]
-    far_peers = [lax.rem(far_me + j, far_count) * group + near_me for j in range(1, far_count)]
+
+    def in_line(distance):
+        return lax.rem(far_me + distance + far_count, far_count) * group + near_me
+
+    near_order = sorted(range(1, group), key=lambda j: -min(j, group - j))
+    far_order = sorted(range(1, far_count), key=lambda j: -min(j, far_count - j))
+    near_peers = [far_me * group + lax.rem(near_me + j, group) for j in near_order]
+    far_peers = [in_line(j) for j in far_order]
 
     barrier = pltpu.get_barrier_semaphore()
-    everyone = [up, down] + near_peers + far_peers
-    for peer in everyone:
+    adjacent = [up, down] + near_peers
+    if far_count > 1:
+        adjacent += [in_line(1), in_line(-1)]
+    for peer in adjacent:
         pl.semaphore_signal(barrier, inc=1, device_id={"col": peer}, device_id_type=MESH)
 
     small_copies = [
@@ -111,7 +120,23 @@
         for level in range(whole, levels):
             yield slice(level, level + 1), pl.ds(level * stride + first, 1)
 
-    def build(step):
+    reaches = []
+    while far_count > 1 and 2 ** len(reaches) < far_count // 2:
+        reaches.append(2 ** len(reaches))
+
+    def announce(turn):
+        if turn < len(reaches):
+            for way, distance in ((0, reaches[turn]), (1, -reaches[turn])):
+                pl.semaphore_signal(
+                    line_sem.at[turn, way], inc=1, device_id={"col": in_line(distance)}, device_id_type=MESH
+                )
+
+    def heard(turn):
+        if 0 <= turn < len(reaches):
+            for way in range(2):
+                pl.semaphore_wait(line_sem.at[turn, way], 1)
+
+    def build(step, first, last):
         points = points_ref[step]
         slot_ids = points // BCOLS
         within = points % BCOLS
@@ -132,9 +157,12 @@
             half = slice(parity * BCOLS, (parity + 1) * BCOLS)
             empty = jnp.zeros((BCOLS, BCOLS), BF16)
             unused = slice(0, BCOLS) if parity else slice(SLOTS * BCOLS, WINDOW)
-            w_high[step, pair, unused, half] = empty
-            w_low[step, pair, unused, half] = empty
+            if first == 0:
+                w_high[step, pair, unused, half] = empty
+                w_low[step, pair, unused, half] = empty
             for piece in range(SLOTS):
+                if not first <= source + piece <= last and not first <= blocks + 3 - source - piece <= last:
+                    continue
                 rows = lax.broadcasted_iota(jnp.int32, (BCOLS, BCOLS), 0) + piece * BCOLS
                 total = jnp.zeros((BCOLS, BCOLS), F32)
                 for point in range(POINTS):
@@ -207,11 +235,14 @@
         for way, tile in ((0, 0), (1, tiles - 1)):
             value = tile_sum(step, diffused, tile)
             for v in range(per_chunk):
-                send_buf[exchange, chunk, way, v] = value[v * padded : (v + 1) * padded]
+                send_buf[exchange, chunk, way, v] = value[v * padded : v * padded + levels]
         if first:
-            pl.semaphore_wait(barrier, len(everyone))
+            pl.semaphore_wait(barrier, len(adjacent))
         for way in range(2):
             halo_copy(exchange, chunk, way).start()
+        if first:
+            announce(0)
+            build(1, 2, 3)
         for tile in range(1, tiles - 1):
             value = tile_sum(step, diffused, tile)
             for v in range(per_chunk):
@@ -224,13 +255,14 @@
             halo_copy(exchange, chunk, way).wait_recv()
         for v in range(per_chunk):
             row = chunk * per_chunk + v
-            own[row, :, 0:PAIR] = own[row, :, 0:PAIR] + recv_buf[exchange, chunk, 1, v]
+            part = slice(0, levels)
+            own[row, part, 0:PAIR] = own[row, part, 0:PAIR] + recv_buf[exchange, chunk, 1, v]
             last = slice(col_count - PAIR, col_count)
-            own[row, :, last] = own[row, :, last] + recv_buf[exchange, chunk, 0, v]
+            own[row, part, last] = own[row, part, last] + recv_buf[exchange, chunk, 0, v]
 
     for copy in small_copies:
         copy.wait()
-    build(1)
+    build(1, 0, 1)
     for copy in inv_copies[1]:
         copy.wait()
     pad_inverse(1)
@@ -254,13 +286,16 @@
 
         scatter(0, 1, chunk, diffused_pairs(block_value, inverses), chunk == 0)
 
-    build(0)
+    build(0, 0, 1)
+    build(0, 2, 3)
     for copy in inv_copies[0]:
         copy.wait()
     pad_inverse(0)
     inverses = [stacked_inverse(source) for source in range(blocks)]
     for chunk in range(CHUNKS):
         arrived(0, chunk)
+        heard(chunk)
+        announce(chunk + 1)
         for v in range(chunk * per_chunk, (chunk + 1) * per_chunk):
             for source in range(blocks):
                 for part, rows in pieces(v, source):
@@ -277,6 +312,10 @@
     total = jnp.zeros((8, BCOLS), F32)
     for chunk in range(CHUNKS):
         arrived(1, chunk)
+        if chunk == 0:
+            for turn in range(CHUNKS, len(reaches)):
+                heard(turn)
+                announce(turn + 1)
         for v in range(chunk * per_chunk, (chunk + 1) * per_chunk):
             value = own[v]
             square = value * value
@@ -304,8 +343,8 @@
         for source in range(blocks):
             for part, rows in pieces(v, source):
                 start_ref[rows, :] = own[v, part, source * BCOLS : (source + 1) * BCOLS]
-    for j, peer in enumerate(near_peers):
-        slot = lax.rem(near_me + j + 1, group)
+    for j, peer in reversed(list(enumerate(near_peers))):
+        slot = lax.rem(near_me + near_order[j], group)
         pltpu.make_async_remote_copy(
             src_ref=near_buf.at[slot],
             dst_ref=near_buf.at[slot],
@@ -331,8 +370,8 @@
     ]
     for copy in far_copies:
         copy.start()
-    for j, peer in enumerate(far_peers):
-        slot = lax.rem(far_me + j + 1, far_count)
+    for j, peer in reversed(list(enumerate(far_peers))):
+        slot = lax.rem(far_me + far_order[j], far_count)
         pltpu.make_async_remote_copy(
             src_ref=far_buf.at[slot],
             dst_ref=far_buf.at[slot],
@@ -374,7 +413,7 @@
     per_chunk = variables // CHUNKS
     group = min(GROUP, count)
     far_count = count // group
-    halo = (2, CHUNKS, 2, per_chunk, padded, PAIR)
+    halo = (2, CHUNKS, 2, per_chunk, levels, PAIR)
     rows = levels * blocks * variables
     like = jax.ShapeDtypeStruct((rows, BCOLS), F32)
     adj_rows = adj_final.reshape(variables, levels, blocks, BCOLS).transpose(1, 2, 0, 3).reshape(rows, BCOLS)
@@ -400,6 +439,7 @@
             pltpu.VMEM(halo, F32),
             pltpu.VMEM((group, 1, BCOLS), F32),
             pltpu.VMEM((far_count, 1, BCOLS), F32),
+            pltpu.SemaphoreType.REGULAR((8, 2)),
             pltpu.SemaphoreType.DMA((3,)),
             pltpu.SemaphoreType.DMA((1,)),
             pltpu.SemaphoreType.DMA((STEPS, blocks)),

time: 43.3 us -> 42.4 us (0.979); the launches traced: 42.6 us -> 42.2 us
  no operation moved by 1% of the time
where the time goes in v3:
time: 42.4 us; the launch traced here: 42.2 us
  Pallas kernels  41.6 us (98%)
  between operations  0.64 us (2%)
    pallas_call x1, Pallas kernels, shards(): pl.pallas_call(functools.partial(kernel, count), out_shape=(like, like, j...  40.2 us
    pallas_call x1, Pallas kernels, shards(): pl.pallas_call(functools.partial(finish, count * adj_final.size), out_sha...  1.38 us

profile of v3, /device:TPU:6, one launch (start us, length us, event | category | flops | bytes accessed | tf_op | source)
XLA Modules:
  0.0 42.2 jit_solution(2000510662805625379)
XLA Ops:
  0.6 40.2 %shard_map.68 = (f32[2192,128]{1,0:T(8,128)S(1)}, f32[2192,128]{1,0:T(8,128)S(1)}, f32[1,128]{1,0:T(1,128)S(1)}) custom-call(s32[2,4,5]{2,1,0:T(4,128)} %lists_hbm.1, s32[2,4,512]{2,1,0:T(4,128)} %points_hbm.1, f32[2,4,512]{2,1,0:T(4,128)} %weights_hbm.1, f32[2192,128]{1,0:T(8,128)} %bitcast.16, f32[2,137,4,137]{3,2,1,0:T(4,128)} %bitcast.17), custom_call_target="tpu_custom_call" | custom-call | tf_op jit(solution)/shard_map/pallas_call | solution.py:422
  40.8 1.4 %shard_map.69 = (f32[2192,128]{1,0:T(8,128)}, f32[2192,128]{1,0:T(8,128)}) custom-call(f32[2192,128]{1,0:T(8,128)S(1)} %get-tuple-element.7.mid_in, f32[2192,128]{1,0:T(8,128)S(1)} %get-tuple-element.8.start_in, f32[1,128]{1,0:T(1,128)S(1)} %get-tuple-element.9.energy_ref), custom_call_target="tpu_custom_call" | custom-call | tf_op jit(solution)/shard_map/pallas_call | solution.py:462

commit v4 on v3

--- a/solution.py
+++ b/solution.py
@@ -17,6 +17,7 @@
 EPS_ENERGY = 1e-06
 GROUP = 8
 CHUNKS = 4
+FINISH_PARTS = 1
 MESH = pl.DeviceIdType.MESH
 F32 = jnp.float32
 BF16 = jnp.bfloat16
@@ -231,7 +232,7 @@
             device_id_type=MESH,
         )
 
-    def scatter(exchange, step, chunk, diffused, first):
+    def scatter(exchange, step, chunk, diffused, first, between):
         for way, tile in ((0, 0), (1, tiles - 1)):
             value = tile_sum(step, diffused, tile)
             for v in range(per_chunk):
@@ -240,9 +241,7 @@
             pl.semaphore_wait(barrier, len(adjacent))
         for way in range(2):
             halo_copy(exchange, chunk, way).start()
-        if first:
-            announce(0)
-            build(1, 2, 3)
+        between()
         for tile in range(1, tiles - 1):
             value = tile_sum(step, diffused, tile)
             for v in range(per_chunk):
@@ -284,7 +283,12 @@
                 [adj_pad[v, :, lanes] for v in range(chunk * per_chunk, (chunk + 1) * per_chunk)], axis=1
             )
 
-        scatter(0, 1, chunk, diffused_pairs(block_value, inverses), chunk == 0)
+        def rest_of_weights(chunk=chunk):
+            if chunk == 0:
+                announce(0)
+                build(1, 2, 3)
+
+        scatter(0, 1, chunk, diffused_pairs(block_value, inverses), chunk == 0, rest_of_weights)
 
     build(0, 0, 1)
     build(0, 2, 3)
@@ -292,30 +296,30 @@
         copy.wait()
     pad_inverse(0)
     inverses = [stacked_inverse(source) for source in range(blocks)]
+    heard(0)
+    announce(1)
     for chunk in range(CHUNKS):
         arrived(0, chunk)
-        heard(chunk)
-        announce(chunk + 1)
-        for v in range(chunk * per_chunk, (chunk + 1) * per_chunk):
-            for source in range(blocks):
-                for part, rows in pieces(v, source):
-                    mid_ref[rows, :] = own[v, part, source * BCOLS : (source + 1) * BCOLS]
-
         def block_value(source, chunk=chunk):
             lanes = slice(source * BCOLS, (source + 1) * BCOLS)
             return jnp.concatenate(
                 [own[v, :, lanes] for v in range(chunk * per_chunk, (chunk + 1) * per_chunk)], axis=1
             )
 
-        scatter(1, 0, chunk, diffused_pairs(block_value, inverses), False)
+        def keep_mid(chunk=chunk):
+            for v in range(chunk * per_chunk, (chunk + 1) * per_chunk):
+                for source in range(blocks):
+                    for part, rows in pieces(v, source):
+                        mid_ref[rows, :] = own[v, part, source * BCOLS : (source + 1) * BCOLS]
+
+        scatter(1, 0, chunk, diffused_pairs(block_value, inverses), False, keep_mid)
+        if chunk == 1:
+            heard(1)
+            announce(2)
 
     total = jnp.zeros((8, BCOLS), F32)
     for chunk in range(CHUNKS):
         arrived(1, chunk)
-        if chunk == 0:
-            for turn in range(CHUNKS, len(reaches)):
-                heard(turn)
-                announce(turn + 1)
         for v in range(chunk * per_chunk, (chunk + 1) * per_chunk):
             value = own[v]
             square = value * value
@@ -331,7 +335,7 @@
             src_ref=near_buf.at[near_me],
             dst_ref=near_buf.at[near_me],
             send_sem=near_send.at[j],
-            recv_sem=near_recv.at[near_me],
+            recv_sem=near_recv.at[0],
             device_id={"col": peer},
             device_id_type=MESH,
         )
@@ -343,46 +347,45 @@
         for source in range(blocks):
             for part, rows in pieces(v, source):
                 start_ref[rows, :] = own[v, part, source * BCOLS : (source + 1) * BCOLS]
-    for j, peer in reversed(list(enumerate(near_peers))):
-        slot = lax.rem(near_me + near_order[j], group)
+    if group > 1:
+        others = pl.ds(0, group - 1)
         pltpu.make_async_remote_copy(
-            src_ref=near_buf.at[slot],
-            dst_ref=near_buf.at[slot],
-            send_sem=near_send.at[j],
-            recv_sem=near_recv.at[slot],
-            device_id={"col": peer},
+            src_ref=near_buf.at[others],
+            dst_ref=near_buf.at[others],
+            send_sem=near_send.at[0],
+            recv_sem=near_recv.at[0],
+            device_id={"col": near_peers[0]},
             device_id_type=MESH,
         ).wait_recv()
-    total = near_buf[0]
-    for slot in range(1, group):
-        total = total + near_buf[slot]
+    total = jnp.sum(near_buf[...], axis=0)
     far_buf[far_me] = total
     far_copies = [
         pltpu.make_async_remote_copy(
             src_ref=far_buf.at[far_me],
             dst_ref=far_buf.at[far_me],
             send_sem=far_send.at[j],
-            recv_sem=far_recv.at[far_me],
+            recv_sem=far_recv.at[0],
             device_id={"col": peer},
             device_id_type=MESH,
         )
         for j, peer in enumerate(far_peers)
     ]
+    for turn in range(2, len(reaches)):
+        heard(turn)
+        announce(turn + 1)
     for copy in far_copies:
         copy.start()
-    for j, peer in reversed(list(enumerate(far_peers))):
-        slot = lax.rem(far_me + far_order[j], far_count)
+    if far_count > 1:
+        others = pl.ds(0, far_count - 1)
         pltpu.make_async_remote_copy(
-            src_ref=far_buf.at[slot],
-            dst_ref=far_buf.at[slot],
-            send_sem=far_send.at[j],
-            recv_sem=far_recv.at[slot],
-            device_id={"col": peer},
+            src_ref=far_buf.at[others],
+            dst_ref=far_buf.at[others],
+            send_sem=far_send.at[0],
+            recv_sem=far_recv.at[0],
+            device_id={"col": far_peers[0]},
             device_id_type=MESH,
         ).wait_recv()
-    total = far_buf[0]
-    for slot in range(1, far_count):
-        total = total + far_buf[slot]
+    total = jnp.sum(far_buf[...], axis=0)
     energy_ref[...] = total
     for exchange in range(2):
         for chunk in range(CHUNKS):
@@ -397,11 +400,16 @@
     mid_copy.start()
     energy = jnp.sum(energy_ref[...], axis=1, keepdims=True)
     scale = 1.0 / jnp.sqrt(energy / cells + EPS_ENERGY)
-    scaled[...] = start_in[...] * scale
-    out_copy = pltpu.make_async_copy(scaled, out_hbm, sem.at[1])
-    out_copy.start()
-    mid_copy.wait()
-    out_copy.wait()
+    size = scaled.shape[0] // FINISH_PARTS
+    copies = [mid_copy]
+    for piece in range(FINISH_PARTS):
+        part = pl.ds(piece * size, size)
+        scaled[part, :] = start_in[part, :] * scale
+        copy = pltpu.make_async_copy(scaled.at[part], out_hbm.at[part], sem.at[1 + piece])
+        copy.start()
+        copies.append(copy)
+    for copy in copies:
+        copy.wait()
 
 
 def shards(adj_final, inverses, dep_lists, dep_points, weights):
@@ -464,7 +472,7 @@
         out_shape=(like, like),
         in_specs=[vmem, vmem, vmem],
         out_specs=(anywhere, anywhere),
-        scratch_shapes=[pltpu.VMEM((rows, BCOLS), F32), pltpu.SemaphoreType.DMA((2,))],
+        scratch_shapes=[pltpu.VMEM((rows, BCOLS), F32), pltpu.SemaphoreType.DMA((1 + FINISH_PARTS,))],
         compiler_params=pltpu.CompilerParams(vmem_limit_bytes=16 << 20),
     )(mid, start, energy)
     return tuple(

time: 42.4 us -> 41.2 us (0.972)
  Pallas kernels: 41.6 us -> 40.4 us
    pallas_call x1, Pallas kernels: 40.2 us -> 39 us  [shards(): pl.pallas_call(functools.partial(kernel, count), out_shape=(like, like, j...]
where the time goes in v4:
time: 41.2 us; the launch traced here: 41 us
  Pallas kernels  40.4 us (98%)
  between operations  0.64 us (2%)
    pallas_call x1, Pallas kernels, shards(): pl.pallas_call(functools.partial(kernel, count), out_shape=(like, like, j...  39 us
    pallas_call x1, Pallas kernels, shards(): pl.pallas_call(functools.partial(finish, count * adj_final.size), out_sha...  1.38 us

profile of v4, /device:TPU:6, one launch (start us, length us, event | category | flops | bytes accessed | tf_op | source)
XLA Modules:
  0.0 41.0 jit_solution(16604008078405497738)
XLA Ops:
  0.6 39.0 %shard_map.68 = (f32[2192,128]{1,0:T(8,128)S(1)}, f32[2192,128]{1,0:T(8,128)S(1)}, f32[1,128]{1,0:T(1,128)S(1)}) custom-call(s32[2,4,5]{2,1,0:T(4,128)} %lists_hbm.1, s32[2,4,512]{2,1,0:T(4,128)} %points_hbm.1, f32[2,4,512]{2,1,0:T(4,128)} %weights_hbm.1, f32[2192,128]{1,0:T(8,128)} %bitcast.16, f32[2,137,4,137]{3,2,1,0:T(4,128)} %bitcast.17), custom_call_target="tpu_custom_call" | custom-call | tf_op jit(solution)/shard_map/pallas_call | solution.py:430
  39.6 1.4 %shard_map.69 = (f32[2192,128]{1,0:T(8,128)}, f32[2192,128]{1,0:T(8,128)}) custom-call(f32[2192,128]{1,0:T(8,128)S(1)} %get-tuple-element.7.mid_in, f32[2192,128]{1,0:T(8,128)S(1)} %get-tuple-element.8.start_in, f32[1,128]{1,0:T(1,128)S(1)} %get-tuple-element.9.energy_ref), custom_call_target="tpu_custom_call" | custom-call | tf_op jit(solution)/shard_map/pallas_call | solution.py:470

commit v5 on v4

--- a/solution.py
+++ b/solution.py
@@ -192,9 +192,9 @@
             preferred_element_type=F32,
         )
 
-    def diffused_pairs(block_value, inverses):
+    def diffused_pairs(block_value, inverses, chosen=None):
         result = []
-        for pair in range(pairs):
+        for pair in range(pairs) if chosen is None else [chosen]:
             left = diffuse(inverses[2 * pair], block_value(2 * pair))
             right = diffuse(inverses[2 * pair + 1], block_value(2 * pair + 1))
             rows = [
@@ -249,15 +249,27 @@
                     v * padded : (v + 1) * padded
                 ]
 
-    def arrived(exchange, chunk):
-        for way in range(2):
-            halo_copy(exchange, chunk, way).wait_recv()
+    def arrived_from(exchange, chunk, way):
+        halo_copy(exchange, chunk, way).wait_recv()
+        part = slice(0, levels)
+        lanes = slice(0, PAIR) if way else slice(col_count - PAIR, col_count)
         for v in range(per_chunk):
             row = chunk * per_chunk + v
-            part = slice(0, levels)
-            own[row, part, 0:PAIR] = own[row, part, 0:PAIR] + recv_buf[exchange, chunk, 1, v]
-            last = slice(col_count - PAIR, col_count)
-            own[row, part, last] = own[row, part, last] + recv_buf[exchange, chunk, 0, v]
+            own[row, part, lanes] = own[row, part, lanes] + recv_buf[exchange, chunk, way, v]
+
+    def send_side(exchange, step, chunk, diffused, way):
+        value = tile_sum(step, diffused, tiles - 1 if way else 0)
+        for v in range(per_chunk):
+            send_buf[exchange, chunk, way, v] = value[v * padded : v * padded + levels]
+        halo_copy(exchange, chunk, way).start()
+
+    def own_tiles(step, chunk, diffused):
+        for tile in range(1, tiles - 1):
+            value = tile_sum(step, diffused, tile)
+            for v in range(per_chunk):
+                own[chunk * per_chunk + v, :, (tile - 1) * PAIR : tile * PAIR] = value[
+                    v * padded : (v + 1) * padded
+                ]
 
     for copy in small_copies:
         copy.wait()
@@ -299,7 +311,6 @@
     heard(0)
     announce(1)
     for chunk in range(CHUNKS):
-        arrived(0, chunk)
         def block_value(source, chunk=chunk):
             lanes = slice(source * BCOLS, (source + 1) * BCOLS)
             return jnp.concatenate(
@@ -312,14 +323,22 @@
                     for part, rows in pieces(v, source):
                         mid_ref[rows, :] = own[v, part, source * BCOLS : (source + 1) * BCOLS]
 
-        scatter(1, 0, chunk, diffused_pairs(block_value, inverses), False, keep_mid)
+        arrived_from(0, chunk, 1)
+        low_side = diffused_pairs(block_value, inverses, 0)
+        send_side(1, 0, chunk, low_side + [None], 0)
+        arrived_from(0, chunk, 0)
+        high_side = diffused_pairs(block_value, inverses, 1)
+        send_side(1, 0, chunk, [None] + high_side, 1)
+        keep_mid()
+        own_tiles(0, chunk, low_side + high_side)
         if chunk == 1:
             heard(1)
             announce(2)
 
     total = jnp.zeros((8, BCOLS), F32)
     for chunk in range(CHUNKS):
-        arrived(1, chunk)
+        for way in (1, 0):
+            arrived_from(1, chunk, way)
         for v in range(chunk * per_chunk, (chunk + 1) * per_chunk):
             value = own[v]
             square = value * value

time: 41.2 us -> 41.3 us (level)
  no operation moved by 1% of the time
where the time goes in v5:
time: 41.3 us; the launch traced here: 41 us
  Pallas kernels  40.3 us (98%)
  between operations  0.64 us (2%)
    pallas_call x1, Pallas kernels, shards(): pl.pallas_call(functools.partial(kernel, count), out_shape=(like, like, j...  39 us
    pallas_call x1, Pallas kernels, shards(): pl.pallas_call(functools.partial(finish, count * adj_final.size), out_sha...  1.38 us

profile of v5, /device:TPU:6, one launch (start us, length us, event | category | flops | bytes accessed | tf_op | source)
XLA Modules:
  0.0 41.0 jit_solution(15585852979469210933)
XLA Ops:
  0.6 39.0 %shard_map.68 = (f32[2192,128]{1,0:T(8,128)S(1)}, f32[2192,128]{1,0:T(8,128)S(1)}, f32[1,128]{1,0:T(1,128)S(1)}) custom-call(s32[2,4,5]{2,1,0:T(4,128)} %lists_hbm.1, s32[2,4,512]{2,1,0:T(4,128)} %points_hbm.1, f32[2,4,512]{2,1,0:T(4,128)} %weights_hbm.1, f32[2192,128]{1,0:T(8,128)} %bitcast.16, f32[2,137,4,137]{3,2,1,0:T(4,128)} %bitcast.17), custom_call_target="tpu_custom_call" | custom-call | tf_op jit(solution)/shard_map/pallas_call | solution.py:449
  39.6 1.4 %shard_map.69 = (f32[2192,128]{1,0:T(8,128)}, f32[2192,128]{1,0:T(8,128)}) custom-call(f32[2192,128]{1,0:T(8,128)S(1)} %get-tuple-element.7.mid_in, f32[2192,128]{1,0:T(8,128)S(1)} %get-tuple-element.8.start_in, f32[1,128]{1,0:T(1,128)S(1)} %get-tuple-element.9.energy_ref), custom_call_target="tpu_custom_call" | custom-call | tf_op jit(solution)/shard_map/pallas_call | solution.py:489
